TPU v7x, 32 devices: a whole 2x2x4 slice. The times are simulated.
32 devices in a mesh: elem: 16 (over z, x, core), band: 2 (over y).
Axes of the slice: x: 2, y: 2, z: 4, core: 2. Of those that a mesh axis runs over, the one named last changes fastest.
Arguments:
- basis: bfloat16 [256, 32, 16, 160], P('band', 'elem'), may hold values from -8 to 8
- hamiltonian: bfloat16 [32, 16, 7, 160, 160], P('elem'), may hold values from -0.09375 to 0.09375
- neighbours: int32 [32, 16, 6], P('elem'), may hold values from 0 to 511, as said below
Outputs:
- filtered: bfloat16 [256, 32, 16, 160], P('band', 'elem')
- intersection: float32 [256, 256], P('elem', 'band')
- projected: float32 [256, 256], P('elem', 'band')
Inputs may be any that keep to these rules, and one draw needn't show every extreme that they name: neighbours[z, s, d] = z2 * 16 + s2 names the element (z2, s2) that shares face d with element (z, s) on a periodic grid of 4 x 4 x 32 cells, whose cells are stored within each layer in an order of the draw; faces 0 to 3 lie in the same layer z, face 4 in layer z - 1 and face 5 in layer z + 1, both modulo 32.
All inputs are finite; a program needn't handle non-finite values.
Results may differ from a plain program's by a relative error of at most 0.0075.
Values may be sent and summed in bfloat16 or wider, within the bound.
A program may use at most 64 MiB of HBM per device.

v0:
```python
import jax
import jax.numpy as jnp
from jax import lax
from jax.sharding import PartitionSpec as P

DEGREE = 4


def extended_2(block, sides, width):
    for axis, dim in sides:
        count = lax.axis_size(axis)
        forward = [(i, i + 1) for i in range(count - 1)]
        forward.append((count - 1, 0))
        backward = [(target, source) for source, target in forward]
        low = lax.ppermute(
            lax.slice_in_dim(block, block.shape[dim] - width, None, axis=dim), axis, forward
        )
        high = lax.ppermute(lax.slice_in_dim(block, 0, width, axis=dim), axis, backward)
        block = jnp.concatenate([low, block, high], axis=dim)
    return block


def body(basis, hamiltonian, neighbours):
    width, layers, cells, functions = basis.shape
    elem_count = lax.axis_size("elem")
    depth = layers * elem_count
    first = lax.axis_index("elem") * layers
    layer_of = neighbours // cells
    relative = (layer_of - first + 1) % depth
    outer = relative * cells + neighbours % cells
    own = (jnp.arange(layers)[:, None] + 1) * cells + jnp.arange(cells)[None, :]
    table = jnp.concatenate([own[:, :, None], outer], axis=2)

    def apply_blocks(field):
        extended = extended_2(field, (("elem", 1),), 1)
        flat = extended.reshape(width, (layers + 2) * cells, functions)
        picked = jnp.take(flat, table, axis=1)
        return jnp.einsum(
            "zsdij,czsdj->czsi", hamiltonian, picked, preferred_element_type=jnp.float32
        )

    previous = basis
    current = apply_blocks(basis).astype(jnp.bfloat16)
    for step in range(DEGREE - 1):
        following = (2.0 * apply_blocks(current) - previous.astype(jnp.float32)).astype(
            jnp.bfloat16
        )
        previous, current = (current, following)
    image = apply_blocks(current).astype(jnp.bfloat16)
    factor = 1.0 / (depth * cells * functions)
    piece = lax.all_gather(current, "band", axis=0, tiled=True)
    left_part = jnp.einsum("kzsi,czsi->kc", piece, current, preferred_element_type=jnp.float32)
    right_part = jnp.einsum("kzsi,czsi->kc", piece, image, preferred_element_type=jnp.float32)
    partial_terms = jnp.stack([left_part, right_part])
    totals = lax.psum_scatter(partial_terms, "elem", scatter_dimension=1, tiled=True)
    return (current, totals[0] * factor, totals[1] * factor)


def solution(mesh):
    placed = (
        P("band", "elem", None, None),
        P("elem", None, None, None, None),
        P("elem", None, None),
    )
    return jax.shard_map(
        body,
        mesh=mesh,
        in_specs=placed,
        out_specs=(P("band", "elem", None, None), P("elem", "band"), P("elem", "band")),
        check_vma=False,
    )
```

profile of v0, /device:TPU:0, one launch (start us, length us, event | category | flops | bytes accessed | tf_op | source)
XLA Modules:
  0.0 281.0 jit_solution(16922853320731717165)
XLA Ops:
  7.2 0.0 copy-start.3
  7.2 0.0 all-gather.2.cloned.1.call-start
  7.2 1.4 fusion.80
  8.6 5.5 %collective-permute-start.1 = (bf16[128,1,16,160]{0,3,2,1:T(8,128)(2,1)S(1)}, bf16[128,1,16,160]{0,3,2,1:T(8,128)(2,1)S(1)}, u32[]{:S(2)}, u32[]{:S(2)}) collective-permute-start(bf16[128,1,16,160]{0,3,2,1:T(8,128)(2,1)S(1)} %get-tuple-element.15), channel_id=1, source_target_pairs={{2,0},{4,2},{6,4},{8,6},{10,8},{12,10},{14,12},{16,14},{18,16},{20... | collective-permute-start | bytes 1966088 | tf_op jit(solution)/shard_map/ppermute | solution.py:18
  14.1 0.0 collective-permute-start
  14.1 0.1 iota_add_fusion
  14.2 0.0 copy-done.3
  14.2 0.1 copy.18
  14.3 0.1 reshape.122
  14.4 0.1 copy.14
  14.6 7.6 %collective-permute-done.1 = bf16[128,1,16,160]{0,3,2,1:T(8,128)(2,1)S(1)} collective-permute-done((bf16[128,1,16,160]{0,3,2,1:T(8,128)(2,1)S(1)}, bf16[128,1,16,160]{0,3,2,1:T(8,128)(2,1)S(1)}, u32[]{:S(2)}, u32[]{:S(2)}) %collective-permute-start.1) | collective-permute-done | bytes 655392 | tf_op jit(solution)/shard_map/ppermute | solution.py:18
  22.2 4.8 %collective-permute-done = bf16[128,1,16,160]{0,3,2,1:T(8,128)(2,1)} collective-permute-done((bf16[128,1,16,160]{0,3,2,1:T(8,128)(2,1)S(1)}, bf16[128,1,16,160]{0,3,2,1:T(8,128)(2,1)}, u32[]{:S(2)}, u32[]{:S(2)}) %collective-permute-start) | collective-permute-done | bytes 655392 | tf_op jit(solution)/shard_map/ppermute | solution.py:15
  27.0 1.8 pad_maximum_fusion
  28.8 9.4 %gather_fusion = bf16[224,128,160]{1,2,0:T(8,128)(2,1)} fusion(bf16[128,64,160]{0,2,1:T(8,128)(2,1)S(1)} %bitcast.108, s32[1024]{0:T(1024)S(1)} %pad_clamp_fusion), kind=kCustom, calls=%fused_computation.clone | custom fusion | bytes 18350976 | tf_op jit(solution)/shard_map/jit(_take)/gather | solution.py:37
  38.2 11.3 %fusion.42 = bf16[128,2,16,160]{0,3,2,1:T(8,128)(2,1)S(1)} fusion(bf16[2,16,7,160,160]{4,3,2,1,0:T(8,128)(2,1)} %param.6, bf16[2,16,7,128,160]{3,4,2,1,0:T(8,128)(2,1)} %bitcast.114, pred[2,16,7]{2,1,0:T(8,128)(4,1)S(1)} %copy.14), kind=kOutput, calls=%fused_computation.49 | convolution fusion | flops 1473249280 | bytes 21954784 | tf_op jit(solution)/shard_map/zsdij,czsdj->czsi/dot_general | solution.py:38
  49.5 0.0 copy-start.2
  49.5 0.1 fusion.79
  49.6 0.1 collective-permute-start.3
  49.7 0.5 collective-permute-start.2
  50.2 7.6 %collective-permute-done.3 = bf16[128,1,16,160]{0,3,2,1:T(8,128)(2,1)S(1)} collective-permute-done((bf16[128,1,16,160]{0,3,2,1:T(8,128)(2,1)S(1)}, bf16[128,1,16,160]{0,3,2,1:T(8,128)(2,1)S(1)}, u32[]{:S(2)}, u32[]{:S(2)}) %collective-permute-start.3) | collective-permute-done | bytes 655392 | tf_op jit(solution)/shard_map/ppermute | solution.py:18
  57.8 5.2 %collective-permute-done.2 = bf16[128,1,16,160]{0,3,2,1:T(8,128)(2,1)S(1)} collective-permute-done((bf16[128,1,16,160]{0,3,2,1:T(8,128)(2,1)S(1)}, bf16[128,1,16,160]{0,3,2,1:T(8,128)(2,1)S(1)}, u32[]{:S(2)}, u32[]{:S(2)}) %collective-permute-start.2) | collective-permute-done | bytes 655392 | tf_op jit(solution)/shard_map/ppermute | solution.py:15
  63.0 0.3 pad_maximum_fusion.1
  63.3 0.0 copy-done.2
  63.3 9.4 %gather_fusion.1 = bf16[224,128,160]{1,2,0:T(8,128)(2,1)} fusion(bf16[128,64,160]{0,2,1:T(8,128)(2,1)S(1)} %bitcast.109, s32[1024]{0:T(1024)S(1)} %pad_clamp_fusion), kind=kCustom, calls=%fused_computation.1.clone | custom fusion | bytes 18350976 | tf_op jit(solution)/shard_map/jit(_take)/gather | solution.py:37
  72.7 11.8 %fusion.25 = bf16[128,2,16,160]{0,3,2,1:T(8,128)(2,1)S(1)} fusion(bf16[128,2,16,160]{0,3,2,1:T(8,128)(2,1)} %param.5, bf16[2,16,7,160,160]{4,3,2,1,0:T(8,128)(2,1)} %param.6, bf16[2,16,7,128,160]{3,4,2,1,0:T(8,128)(2,1)} %bitcast.115, pred[2,16,7]{2,1,0:T(8,128)(4,1)S(1)} %copy.14), kind=kOutput, calls=%fused_computation.42 | convolution fusion | flops 1475215360 | bytes 23265504 | tf_op jit(solution)/shard_map/zsdij,czsdj->czsi/dot_general | solution.py:38
  84.5 0.0 copy-start.1
  84.6 0.1 fusion.78
  84.7 0.1 collective-permute-start.5
  84.7 3.9 %collective-permute-start.4 = (bf16[128,1,16,160]{0,3,2,1:T(8,128)(2,1)S(1)}, bf16[128,1,16,160]{0,3,2,1:T(8,128)(2,1)S(1)}, u32[]{:S(2)}, u32[]{:S(2)}) collective-permute-start(bf16[128,1,16,160]{0,3,2,1:T(8,128)(2,1)S(1)} %get-tuple-element.10), channel_id=1, source_target_pairs={{0,2},{2,4},{4,6},{6,8},{8,10},{10,12},{12,14},{14,16},{16,18},{18... | collective-permute-start | bytes 1966088 | tf_op jit(solution)/shard_map/ppermute | solution.py:15
  88.7 4.2 %collective-permute-done.5 = bf16[128,1,16,160]{0,3,2,1:T(8,128)(2,1)S(1)} collective-permute-done((bf16[128,1,16,160]{0,3,2,1:T(8,128)(2,1)S(1)}, bf16[128,1,16,160]{0,3,2,1:T(8,128)(2,1)S(1)}, u32[]{:S(2)}, u32[]{:S(2)}) %collective-permute-start.5) | collective-permute-done | bytes 655392 | tf_op jit(solution)/shard_map/ppermute | solution.py:18
  92.8 7.4 %collective-permute-done.4 = bf16[128,1,16,160]{0,3,2,1:T(8,128)(2,1)S(1)} collective-permute-done((bf16[128,1,16,160]{0,3,2,1:T(8,128)(2,1)S(1)}, bf16[128,1,16,160]{0,3,2,1:T(8,128)(2,1)S(1)}, u32[]{:S(2)}, u32[]{:S(2)}) %collective-permute-start.4) | collective-permute-done | bytes 655392 | tf_op jit(solution)/shard_map/ppermute | solution.py:15
  100.2 0.3 pad_maximum_fusion.2
  100.5 0.0 copy-done.1
  100.5 9.4 %gather_fusion.2 = bf16[224,128,160]{1,2,0:T(8,128)(2,1)} fusion(bf16[128,64,160]{0,2,1:T(8,128)(2,1)S(1)} %bitcast.110, s32[1024]{0:T(1024)S(1)} %pad_clamp_fusion), kind=kCustom, calls=%fused_computation.2.clone | custom fusion | bytes 18350976 | tf_op jit(solution)/shard_map/jit(_take)/gather | solution.py:37
  109.9 11.8 %fusion.24 = bf16[128,2,16,160]{0,3,2,1:T(8,128)(2,1)S(1)} fusion(bf16[128,2,16,160]{0,3,2,1:T(8,128)(2,1)} %copy-done.2, bf16[2,16,7,160,160]{4,3,2,1,0:T(8,128)(2,1)} %param.6, bf16[2,16,7,128,160]{3,4,2,1,0:T(8,128)(2,1)} %bitcast.112, pred[2,16,7]{2,1,0:T(8,128)(4,1)S(1)} %copy.14), kind=kOutput, calls=%fused_computation.39 | convolution fusion | flops 1475215360 | bytes 23265504 | tf_op jit(solution)/shard_map/zsdij,czsdj->czsi/dot_general | solution.py:38
  121.7 0.1 fusion.77
  121.8 0.1 collective-permute-start.7
  121.9 5.7 %collective-permute-start.6 = (bf16[128,1,16,160]{0,3,2,1:T(8,128)(2,1)S(1)}, bf16[128,1,16,160]{0,3,2,1:T(8,128)(2,1)S(1)}, u32[]{:S(2)}, u32[]{:S(2)}) collective-permute-start(bf16[128,1,16,160]{0,3,2,1:T(8,128)(2,1)S(1)} %get-tuple-element.8), channel_id=1, source_target_pairs={{0,2},{2,4},{4,6},{6,8},{8,10},{10,12},{12,14},{14,16},{16,18},{18... | collective-permute-start | bytes 1966088 | tf_op jit(solution)/shard_map/ppermute | solution.py:15
  127.6 2.4 collective-permute-done.7
  130.0 6.1 %collective-permute-done.6 = bf16[128,1,16,160]{0,3,2,1:T(8,128)(2,1)S(1)} collective-permute-done((bf16[128,1,16,160]{0,3,2,1:T(8,128)(2,1)S(1)}, bf16[128,1,16,160]{0,3,2,1:T(8,128)(2,1)S(1)}, u32[]{:S(2)}, u32[]{:S(2)}) %collective-permute-start.6) | collective-permute-done | bytes 655392 | tf_op jit(solution)/shard_map/ppermute | solution.py:15
  136.1 0.3 pad_maximum_fusion.3
  136.4 9.4 %gather_fusion.3 = bf16[224,128,160]{1,2,0:T(8,128)(2,1)} fusion(bf16[128,64,160]{0,2,1:T(8,128)(2,1)S(1)} %bitcast.106, s32[1024]{0:T(1024)S(1)} %pad_clamp_fusion), kind=kCustom, calls=%fused_computation.3.clone | custom fusion | bytes 18350976 | tf_op jit(solution)/shard_map/jit(_take)/gather | solution.py:37
  145.8 12.9 %fusion.23 = bf16[128,2,16,160]{0,3,2,1:T(8,128)(2,1)} fusion(bf16[128,2,16,160]{0,3,2,1:T(8,128)(2,1)} %copy-done.1, bf16[2,16,7,160,160]{4,3,2,1,0:T(8,128)(2,1)} %param.6, bf16[2,16,7,128,160]{3,4,2,1,0:T(8,128)(2,1)} %bitcast.113, pred[2,16,7]{2,1,0:T(8,128)(4,1)S(1)} %copy.14), kind=kOutput, calls=%fused_computation.36 | convolution fusion | flops 1475215360 | bytes 23265504 | tf_op jit(solution)/shard_map/zsdij,czsdj->czsi/dot_general | solution.py:38
  158.6 0.0 all-gather.2.cloned.1.call-update
  158.7 0.0 reduce-scatter.2.cloned.1.call-start
  158.7 0.0 copy-start
  158.7 1.5 fusion.76
  160.2 0.1 collective-permute-start.9
  160.3 6.8 %collective-permute-start.8 = (bf16[128,1,16,160]{0,3,2,1:T(8,128)(2,1)S(1)}, bf16[128,1,16,160]{0,3,2,1:T(8,128)(2,1)S(1)}, u32[]{:S(2)}, u32[]{:S(2)}) collective-permute-start(bf16[128,1,16,160]{0,3,2,1:T(8,128)(2,1)S(1)} %get-tuple-element.6), channel_id=1, source_target_pairs={{0,2},{2,4},{4,6},{6,8},{8,10},{10,12},{12,14},{14,16},{16,18},{18... | collective-permute-start | bytes 1966088 | tf_op jit(solution)/shard_map/ppermute | solution.py:15
  167.1 1.5 collective-permute-done.9
  168.6 6.5 %collective-permute-done.8 = bf16[128,1,16,160]{0,3,2,1:T(8,128)(2,1)S(1)} collective-permute-done((bf16[128,1,16,160]{0,3,2,1:T(8,128)(2,1)S(1)}, bf16[128,1,16,160]{0,3,2,1:T(8,128)(2,1)S(1)}, u32[]{:S(2)}, u32[]{:S(2)}) %collective-permute-start.8) | collective-permute-done | bytes 655392 | tf_op jit(solution)/shard_map/ppermute | solution.py:15
  175.1 0.0 copy-done
  175.1 0.3 pad_maximum_fusion.4
  175.4 9.4 %gather_fusion.4 = bf16[224,128,160]{1,2,0:T(8,128)(2,1)} fusion(bf16[128,64,160]{0,2,1:T(8,128)(2,1)S(1)} %bitcast.107, s32[1024]{0:T(1024)S(1)} %pad_clamp_fusion), kind=kCustom, calls=%fused_computation.4.clone | custom fusion | bytes 18350976 | tf_op jit(solution)/shard_map/jit(_take)/gather | solution.py:37
  184.8 17.0 %all-gather.2.cloned.1.call-done = bf16[256,2,16,160]{0,3,2,1:T(8,128)(2,1)} async-done(((bf16[128,2,16,160]{0,3,2,1:T(8,128)(2,1)}), bf16[256,2,16,160]{0,3,2,1:T(8,128)(2,1)}) %all-gather.2.cloned.1.call-update) | async-done | bytes 2621456 | tf_op jit(solution)/shard_map/all_gather | solution.py:51
  201.8 0.0 copy-start.4
  201.8 3.1 %fusion.55 = f32[1,256,128]{2,1,0:T(8,128)S(1)} fusion(bf16[128,2,16,160]{0,3,2,1:T(8,128)(2,1)} %fusion.23, bf16[256,2,16,160]{0,3,2,1:T(8,128)(2,1)} %all-gather.2.cloned.1.call-done), kind=kOutput, calls=%fused_computation.52 | convolution fusion | flops 335544320 | bytes 4063232 | tf_op jit(solution)/shard_map/kzsi,czsi->kc/dot_general | solution.py:52
  205.0 0.0 copy-done.4
  205.0 11.3 %fusion.60 = f32[1,256,128]{2,1,0:T(8,128)S(1)} fusion(bf16[2,16,7,160,160]{4,3,2,1,0:T(8,128)(2,1)} %param.6, bf16[256,2,16,160]{0,3,2,1:T(8,128)(2,1)S(1)} %copy-done.4, bf16[2,16,7,128,160]{3,4,2,1,0:T(8,128)(2,1)} %bitcast.111, pred[2,16,7]{2,1,0:T(8,128)(4,1)S(1)} %copy.14), kind=kOutput, calls=%fused_computation.53 | convolution fusion | flops 1808793600 | bytes 23396576 | tf_op jit(solution)/shard_map/kzsi,czsi->kc/dot_general | solution.py:53
  216.2 0.7 pad_maximum_fusion.5
  217.0 0.0 reduce-scatter.2.cloned.1.call-update
  217.0 55.9 %reduce-scatter.2.cloned.1.call-done = f32[2,16,128]{2,1,0:T(8,128)} async-done(((f32[2,256,128]{2,1,0:T(8,128)}), f32[2,16,128]{2,1,0:T(8,128)}) %reduce-scatter.2.cloned.1.call-update) | async-done | bytes 16400 | tf_op jit(solution)/shard_map/reduce_scatter | solution.py:55
  272.9 1.3 fusion.67
  (4 shorter events, 0.1 us)
Async XLA Ops:
  7.2 7.0 %copy-start.3 = (s32[2,16,6]{1,0,2:T(2,128)S(1)}, s32[2,16,6]{1,0,2:T(2,128)}, u32[]{:S(2)}) copy-start(s32[2,16,6]{1,0,2:T(2,128)} %param.7) | copy-start | bytes 2308
  7.2 194.6 %all-gather.2.cloned.1.call-start = ((), (), s32[]{:S(2)}) async-start(), calls=%async_computation.1 | async-start | bytes 3932160 | tf_op jit(solution)/shard_map/all_gather | solution.py:51
  8.6 13.6 %collective-permute-start.1 = (bf16[128,1,16,160]{0,3,2,1:T(8,128)(2,1)S(1)}, bf16[128,1,16,160]{0,3,2,1:T(8,128)(2,1)S(1)}, u32[]{:S(2)}, u32[]{:S(2)}) collective-permute-start(bf16[128,1,16,160]{0,3,2,1:T(8,128)(2,1)S(1)} %get-tuple-element.15), channel_id=1, source_target_pairs={{2,0},{4,2},{6,4},{8,6},{10,8},{12,10},{14,12},{16,14},{18,16},{20... | collective-permute-start | bytes 1966088 | tf_op jit(solution)/shard_map/ppermute | solution.py:18
  14.1 12.9 %collective-permute-start = (bf16[128,1,16,160]{0,3,2,1:T(8,128)(2,1)S(1)}, bf16[128,1,16,160]{0,3,2,1:T(8,128)(2,1)}, u32[]{:S(2)}, u32[]{:S(2)}) collective-permute-start(bf16[128,1,16,160]{0,3,2,1:T(8,128)(2,1)S(1)} %get-tuple-element.14), channel_id=1, source_target_pairs={{0,2},{2,4},{4,6},{6,8},{8,10},{10,12},{12,14},{14,16},{16,18},{18... | collective-permute-start | bytes 1966088 | tf_op jit(solution)/shard_map/ppermute | solution.py:15
  49.5 13.8 %copy-start.2 = (bf16[128,2,16,160]{0,3,2,1:T(8,128)(2,1)}, bf16[128,2,16,160]{0,3,2,1:T(8,128)(2,1)S(1)}, u32[]{:S(2)}) copy-start(bf16[128,2,16,160]{0,3,2,1:T(8,128)(2,1)S(1)} %fusion.42) | copy-start | bytes 3932164
  49.6 8.2 %collective-permute-start.3 = (bf16[128,1,16,160]{0,3,2,1:T(8,128)(2,1)S(1)}, bf16[128,1,16,160]{0,3,2,1:T(8,128)(2,1)S(1)}, u32[]{:S(2)}, u32[]{:S(2)}) collective-permute-start(bf16[128,1,16,160]{0,3,2,1:T(8,128)(2,1)S(1)} %get-tuple-element.13), channel_id=1, source_target_pairs={{2,0},{4,2},{6,4},{8,6},{10,8},{12,10},{14,12},{16,14},{18,16},{20... | collective-permute-start | bytes 1966088 | tf_op jit(solution)/shard_map/ppermute | solution.py:18
  49.7 13.3 %collective-permute-start.2 = (bf16[128,1,16,160]{0,3,2,1:T(8,128)(2,1)S(1)}, bf16[128,1,16,160]{0,3,2,1:T(8,128)(2,1)S(1)}, u32[]{:S(2)}, u32[]{:S(2)}) collective-permute-start(bf16[128,1,16,160]{0,3,2,1:T(8,128)(2,1)S(1)} %get-tuple-element.12), channel_id=1, source_target_pairs={{0,2},{2,4},{4,6},{6,8},{8,10},{10,12},{12,14},{14,16},{16,18},{18... | collective-permute-start | bytes 1966088 | tf_op jit(solution)/shard_map/ppermute | solution.py:15
  84.5 15.9 %copy-start.1 = (bf16[128,2,16,160]{0,3,2,1:T(8,128)(2,1)}, bf16[128,2,16,160]{0,3,2,1:T(8,128)(2,1)S(1)}, u32[]{:S(2)}) copy-start(bf16[128,2,16,160]{0,3,2,1:T(8,128)(2,1)S(1)} %fusion.25) | copy-start | bytes 3932164
  84.7 8.2 %collective-permute-start.5 = (bf16[128,1,16,160]{0,3,2,1:T(8,128)(2,1)S(1)}, bf16[128,1,16,160]{0,3,2,1:T(8,128)(2,1)S(1)}, u32[]{:S(2)}, u32[]{:S(2)}) collective-permute-start(bf16[128,1,16,160]{0,3,2,1:T(8,128)(2,1)S(1)} %get-tuple-element.11), channel_id=1, source_target_pairs={{2,0},{4,2},{6,4},{8,6},{10,8},{12,10},{14,12},{16,14},{18,16},{20... | collective-permute-start | bytes 1966088 | tf_op jit(solution)/shard_map/ppermute | solution.py:18
  84.7 15.5 %collective-permute-start.4 = (bf16[128,1,16,160]{0,3,2,1:T(8,128)(2,1)S(1)}, bf16[128,1,16,160]{0,3,2,1:T(8,128)(2,1)S(1)}, u32[]{:S(2)}, u32[]{:S(2)}) collective-permute-start(bf16[128,1,16,160]{0,3,2,1:T(8,128)(2,1)S(1)} %get-tuple-element.10), channel_id=1, source_target_pairs={{0,2},{2,4},{4,6},{6,8},{8,10},{10,12},{12,14},{14,16},{16,18},{18... | collective-permute-start | bytes 1966088 | tf_op jit(solution)/shard_map/ppermute | solution.py:15
  121.8 8.2 %collective-permute-start.7 = (bf16[128,1,16,160]{0,3,2,1:T(8,128)(2,1)S(1)}, bf16[128,1,16,160]{0,3,2,1:T(8,128)(2,1)S(1)}, u32[]{:S(2)}, u32[]{:S(2)}) collective-permute-start(bf16[128,1,16,160]{0,3,2,1:T(8,128)(2,1)S(1)} %get-tuple-element.9), channel_id=1, source_target_pairs={{2,0},{4,2},{6,4},{8,6},{10,8},{12,10},{14,12},{16,14},{18,16},{20... | collective-permute-start | bytes 1966088 | tf_op jit(solution)/shard_map/ppermute | solution.py:18
  121.9 14.2 %collective-permute-start.6 = (bf16[128,1,16,160]{0,3,2,1:T(8,128)(2,1)S(1)}, bf16[128,1,16,160]{0,3,2,1:T(8,128)(2,1)S(1)}, u32[]{:S(2)}, u32[]{:S(2)}) collective-permute-start(bf16[128,1,16,160]{0,3,2,1:T(8,128)(2,1)S(1)} %get-tuple-element.8), channel_id=1, source_target_pairs={{0,2},{2,4},{4,6},{6,8},{8,10},{10,12},{12,14},{14,16},{16,18},{18... | collective-permute-start | bytes 1966088 | tf_op jit(solution)/shard_map/ppermute | solution.py:15
  158.7 114.2 %reduce-scatter.2.cloned.1.call-start = ((), (), s32[]{:S(2)}) async-start(), calls=%async_computation.2 | async-start | bytes 278528 | tf_op jit(solution)/shard_map/reduce_scatter | solution.py:55
  158.7 16.4 %copy-start = (bf16[128,2,16,160]{0,3,2,1:T(8,128)(2,1)S(1)}, bf16[128,2,16,160]{0,3,2,1:T(8,128)(2,1)}, u32[]{:S(2)}) copy-start(bf16[128,2,16,160]{0,3,2,1:T(8,128)(2,1)} %fusion.23) | copy-start | bytes 3932164
  160.2 8.4 %collective-permute-start.9 = (bf16[128,1,16,160]{0,3,2,1:T(8,128)(2,1)S(1)}, bf16[128,1,16,160]{0,3,2,1:T(8,128)(2,1)S(1)}, u32[]{:S(2)}, u32[]{:S(2)}) collective-permute-start(bf16[128,1,16,160]{0,3,2,1:T(8,128)(2,1)S(1)} %get-tuple-element.7), channel_id=1, source_target_pairs={{2,0},{4,2},{6,4},{8,6},{10,8},{12,10},{14,12},{16,14},{18,16},{20... | collective-permute-start | bytes 1966088 | tf_op jit(solution)/shard_map/ppermute | solution.py:18
  160.3 14.8 %collective-permute-start.8 = (bf16[128,1,16,160]{0,3,2,1:T(8,128)(2,1)S(1)}, bf16[128,1,16,160]{0,3,2,1:T(8,128)(2,1)S(1)}, u32[]{:S(2)}, u32[]{:S(2)}) collective-permute-start(bf16[128,1,16,160]{0,3,2,1:T(8,128)(2,1)S(1)} %get-tuple-element.6), channel_id=1, source_target_pairs={{0,2},{2,4},{4,6},{6,8},{8,10},{10,12},{12,14},{14,16},{16,18},{18... | collective-permute-start | bytes 1966088 | tf_op jit(solution)/shard_map/ppermute | solution.py:15
  201.8 3.1 %copy-start.4 = (bf16[256,2,16,160]{0,3,2,1:T(8,128)(2,1)S(1)}, bf16[256,2,16,160]{0,3,2,1:T(8,128)(2,1)}, u32[]{:S(2)}) copy-start(bf16[256,2,16,160]{0,3,2,1:T(8,128)(2,1)} %all-gather.2.cloned.1.call-done) | copy-start | bytes 7864324
Sparse Core Ops, SparseCore 0:
  158.8 42.9 all-gather.1
  217.1 55.7 reduce-scatter.1
where the time goes:
time: 281 us
  waiting for transfers between devices  126 us (45%)
  matrix products  62.2 us (22%)
  local copies, waits for them, and re-layouts  50.4 us (18%)
  starting transfers between devices  22.8 us (8%)
  between operations  14.2 us (5%)
  other arithmetic  5.15 us (2%)
    reduce_scatter x1, waiting for transfers between devices, body(): lax.psum_scatter(partial_terms, 'elem', scatter_dimension=1, tiled=True)  55.9 us
    dot_general x4, matrix products, apply_blocks(): jnp.einsum('zsdij,czsdj->czsi', hamiltonian, picked, preferred_element_ty...  47.8 us
    gather x5, local copies, waits for them, and re-layouts, apply_blocks(): picked = jnp.take(flat, table, axis=1)  47 us
    ppermute x5, waiting for transfers between devices, extended_2(): lax.ppermute(lax.slice_in_dim(block, block.shape[dim] - width, None, axis...  30 us
    ppermute x5, waiting for transfers between devices, extended_2(): lax.ppermute(lax.slice_in_dim(block, 0, width, axis=dim), axis, backward)  23.3 us
    all_gather x1, waiting for transfers between devices, body(): piece = lax.all_gather(current, 'band', axis=0, tiled=True)  17 us
    ppermute x5, starting transfers between devices, extended_2(): lax.ppermute(lax.slice_in_dim(block, block.shape[dim] - width, None, axis...  17 us
    dot_general x1, matrix products, body(): jnp.einsum('kzsi,czsi->kc', piece, image, preferred_element_type=jnp.floa...  11.3 us
  transfers between devices with their start and end apart: 12, of which 12 were waited for; matrix products, arithmetic and copies ran while one was open for 4% of the time, Pallas kernels for 0%

commit v1 on v0

v1 whole, which is shorter than its diff:
```python
import functools

import jax
import jax.numpy as jnp
from jax import lax
from jax.experimental import pallas as pl
from jax.experimental.pallas import tpu as pltpu
from jax.sharding import PartitionSpec as P

DEGREE = 4
MESH = pl.DeviceIdType.MESH
F32 = jnp.float32
BF16 = jnp.bfloat16


def dot(a, b):
    return jnp.dot(a, b, preferred_element_type=F32)


def kernel(
    geom,
    tab,
    y0,
    ham_hbm,
    ft,
    s_out,
    p_out,
    ham,
    buf_a,
    buf_b,
    lo0,
    lo1,
    hi0,
    hi1,
    acc,
    it,
    others,
    parts,
    got1,
    mid,
    got2,
    ham_sem,
    send_sem,
    recv_sem,
    fsend,
    frecv,
    r1send,
    r1recv,
    r2send,
    r2recv,
):
    n, nband, cells, n1, n2, rows, factor = geom
    total = 2 * cells
    funcs, bands = y0.shape[1], y0.shape[2]
    me = lax.axis_index("elem")
    bme = lax.axis_index("band")
    right, left = lax.rem(me + 1, n), lax.rem(me + n - 1, n)
    group, member = me // n1, me % n1

    hcopies = []
    hparts = ham_sem.shape[0]
    for c in range(hparts):
        size = ham.shape[0] // hparts
        window = pl.ds(c * size, size)
        hc = pltpu.make_async_copy(ham_hbm.at[window], ham.at[window], ham_sem.at[c])
        hc.start()
        hcopies.append(hc)

    barrier = pltpu.get_barrier_semaphore()
    peers = [{"elem": left}, {"elem": right}]
    for j in range(1, nband):
        peers.append({"band": lax.rem(bme + j, nband)})
    for j in range(1, n1):
        peers.append({"elem": group * n1 + lax.rem(member + j, n1)})
    for j in range(1, n2):
        peers.append({"elem": lax.rem(group + j, n2) * n1 + member})
    for peer in peers:
        pl.semaphore_signal(barrier, inc=1, device_id=peer, device_id_type=MESH)
    pl.semaphore_wait(barrier, len(peers))

    los, his = (lo0, lo1), (hi0, hi1)

    def send_up(step, source):
        copy = pltpu.make_async_remote_copy(
            src_ref=source.at[pl.ds(cells, cells)],
            dst_ref=los[step % 2],
            send_sem=send_sem.at[step, 0],
            recv_sem=recv_sem.at[step, 0],
            device_id={"elem": right},
            device_id_type=MESH,
        )
        copy.start()
        return copy

    def send_down(step, source):
        copy = pltpu.make_async_remote_copy(
            src_ref=source.at[pl.ds(0, cells)],
            dst_ref=his[step % 2],
            send_sem=send_sem.at[step, 1],
            recv_sem=recv_sem.at[step, 1],
            device_id={"elem": left},
            device_id_type=MESH,
        )
        copy.start()
        return copy

    fcopies = []

    def send_field(layer):
        window = pl.ds(layer * cells, cells)
        for j in range(1, nband):
            copy = pltpu.make_async_remote_copy(
                src_ref=buf_a.at[window],
                dst_ref=others.at[j - 1, window],
                send_sem=fsend.at[j - 1, layer],
                recv_sem=frecv.at[j - 1, layer],
                device_id={"band": lax.rem(bme + j, nband)},
                device_id_type=MESH,
            )
            copy.start()
            fcopies.append((j, layer, copy))

    up, down = send_up(0, y0), send_down(0, y0)
    for hc in hcopies:
        hc.wait()

    current = y0
    for step in range(DEGREE + 1):
        last = step == DEGREE
        target = buf_b if step % 2 == 0 else buf_a
        prior = y0 if step == 1 else target

        def local(e, carry, current=current):
            six = e // cells
            base = e * 7
            total_ = dot(ham[base], current[e])
            for d in range(4):
                total_ += dot(ham[base + d + 1], current[tab[e * 6 + d]])
            total_ += dot(ham[base + 6 - six], current[tab[e * 6 + 4]])
            acc[e] = total_
            return carry

        lax.fori_loop(0, total, local, 0)

        def finish(e, carry, step=step, halo=None, face=0, target=target, prior=prior):
            value = acc[e] + dot(ham[e * 7 + face], halo[tab[e * 6 + 5]])
            if step > 0 and step < DEGREE:
                value = 2.0 * value - prior[e].astype(F32)
            if step < DEGREE:
                target[e] = value.astype(BF16)
            if step == DEGREE:
                it[e] = value.T.astype(BF16)
            return carry

        up_next = down_next = None
        down.wait_recv()
        lax.fori_loop(
            cells, total, functools.partial(finish, halo=his[step % 2], face=6), 0
        )
        if not last:
            up_next = send_up(step + 1, target)
        if step == DEGREE - 1:
            send_field(1)
        up.wait_recv()
        lax.fori_loop(
            0, cells, functools.partial(finish, halo=los[step % 2], face=5), 0
        )
        if not last:
            down_next = send_down(step + 1, target)
        if step == DEGREE - 1:
            send_field(0)

            def turn(e, carry):
                ft[e] = buf_a[e].astype(F32).T.astype(BF16)
                return carry

            lax.fori_loop(0, total, turn, 0)
        up.wait_send()
        down.wait_send()
        up, down = up_next, down_next
        current = target

    per = bands // rows

    def gram(field, first, count, state):
        def body(e, carry):
            s, p = carry
            v = field(e)
            return s + dot(ft[e], v), p + dot(it[e], v)

        return lax.fori_loop(first, first + count, body, state)

    def put(who, state):
        for t in range(2):
            block = state[t].T.reshape(per, rows, bands)
            for i in range(per):
                r = who * per + i
                parts[r % n1, r // n1, t] = block[i]

    zero = jnp.zeros((bands, bands), F32)
    put(bme, gram(lambda e: buf_a[e], 0, total, (zero, zero)))
    for j in range(1, nband):
        state = (zero, zero)
        for jj, layer, copy in fcopies:
            if jj == j:
                copy.wait_recv()
                state = gram(lambda e: others[j - 1, e], layer * cells, cells, state)
        put(lax.rem(bme + nband - j, nband), state)

    copies = []
    for j in range(1, n1):
        to = lax.rem(member + j, n1)
        copy = pltpu.make_async_remote_copy(
            src_ref=parts.at[to],
            dst_ref=got1.at[j - 1],
            send_sem=r1send.at[j - 1],
            recv_sem=r1recv.at[j - 1],
            device_id={"elem": group * n1 + to},
            device_id_type=MESH,
        )
        copy.start()
        copies.append(copy)
    for _, _, copy in fcopies:
        copy.wait_send()
    running = parts[member]
    for j, copy in enumerate(copies):
        copy.wait_recv()
        running += got1[j]
    mid[...] = running
    copies2 = []
    for j in range(1, n2):
        to = lax.rem(group + j, n2)
        copy = pltpu.make_async_remote_copy(
            src_ref=mid.at[to],
            dst_ref=got2.at[j - 1],
            send_sem=r2send.at[j - 1],
            recv_sem=r2recv.at[j - 1],
            device_id={"elem": to * n1 + member},
            device_id_type=MESH,
        )
        copy.start()
        copies2.append(copy)
    for copy in copies:
        copy.wait_send()
    final = mid[group]
    for j, copy in enumerate(copies2):
        copy.wait_recv()
        final += got2[j]
    for copy in copies2:
        copy.wait_send()
    s_out[...] = final[0] * factor
    p_out[...] = final[1] * factor


def body(n, nband, basis, hamiltonian, neighbours):
    bands, layers, cells, funcs = basis.shape
    total = layers * cells
    depth = layers * n
    rows = bands * nband // n
    n1 = 4
    n2 = n // n1
    first = lax.axis_index("elem") * layers
    layer_of = neighbours // cells
    cell_of = neighbours % cells
    inside = (layer_of - first) % depth * cells + cell_of
    low = jnp.concatenate([inside[0, :, :4], inside[0, :, 5:6], cell_of[0, :, 4:5]], axis=1)
    high = jnp.concatenate([inside[1, :, :4], inside[1, :, 4:5], cell_of[1, :, 5:6]], axis=1)
    tab = jnp.concatenate([low, high], axis=0).reshape(-1)
    y0 = basis.reshape(bands, total, funcs).transpose(1, 2, 0)
    ham = hamiltonian.reshape(total * 7, funcs, funcs)
    factor = 1.0 / (depth * cells * funcs)
    geom = (n, nband, cells, n1, n2, rows, factor)
    vm = pl.BlockSpec(memory_space=pltpu.VMEM)
    half = (cells, funcs, bands)
    dma = pltpu.SemaphoreType.DMA
    small = jax.ShapeDtypeStruct((rows, bands), F32)
    ft, s, p = pl.pallas_call(
        functools.partial(kernel, geom),
        out_shape=(jax.ShapeDtypeStruct((total, bands, funcs), BF16), small, small),
        in_specs=[
            pl.BlockSpec(memory_space=pltpu.SMEM),
            vm,
            pl.BlockSpec(memory_space=pl.ANY),
        ],
        out_specs=(vm, vm, vm),
        scratch_shapes=[
            pltpu.VMEM((total * 7, funcs, funcs), BF16),
            pltpu.VMEM((total, funcs, bands), BF16),
            pltpu.VMEM((total, funcs, bands), BF16),
            pltpu.VMEM(half, BF16),
            pltpu.VMEM(half, BF16),
            pltpu.VMEM(half, BF16),
            pltpu.VMEM(half, BF16),
            pltpu.VMEM((total, funcs, bands), F32),
            pltpu.VMEM((total, bands, funcs), BF16),
            pltpu.VMEM((nband - 1, total, funcs, bands), BF16),
            pltpu.VMEM((n1, n2, 2, rows, bands), F32),
            pltpu.VMEM((n1 - 1, n2, 2, rows, bands), F32),
            pltpu.VMEM((n2, 2, rows, bands), F32),
            pltpu.VMEM((n2 - 1, 2, rows, bands), F32),
            dma((4,)),
            dma((DEGREE + 1, 2)),
            dma((DEGREE + 1, 2)),
            dma((nband - 1, 2)),
            dma((nband - 1, 2)),
            dma((n1 - 1,)),
            dma((n1 - 1,)),
            dma((n2 - 1,)),
            dma((n2 - 1,)),
        ],
        compiler_params=pltpu.CompilerParams(
            collective_id=0, has_side_effects=True, vmem_limit_bytes=56 * 1024 * 1024
        ),
    )(tab, y0, ham)
    filtered = ft.transpose(1, 0, 2).reshape(bands, layers, cells, funcs)
    return filtered, s, p


def solution(mesh):
    placed = (
        P("band", "elem", None, None),
        P("elem", None, None, None, None),
        P("elem", None, None),
    )
    return jax.shard_map(
        functools.partial(body, mesh.shape["elem"], mesh.shape["band"]),
        mesh=mesh,
        in_specs=placed,
        out_specs=(P("band", "elem", None, None), P("elem", "band"), P("elem", "band")),
        check_vma=False,
    )
```

time: 281 us -> 123 us (0.44)
  waiting for transfers between devices: 126 us -> 0 us
  Pallas kernels: 0 us -> 115 us
  matrix products: 62.2 us -> 0 us
  local copies, waits for them, and re-layouts: 50.4 us -> 5.73 us
  starting transfers between devices: 22.8 us -> 0 us
  between operations: 14.2 us -> 0.68 us
  other arithmetic: 5.15 us -> 0.81 us
    pallas_call x0 -> x1, Pallas kernels: none -> 115 us  [body(): pl.pallas_call(functools.partial(kernel, geom), out_shape=(jax.ShapeDtype...]
    dot_general x6 -> x0, matrix products: 62.2 us -> none  [the longest x4 47.8 us: apply_blocks(): jnp.einsum('zsdij,czsdj->czsi', hamiltonian, picked, preferred_element_ty...]
    reduce_scatter x1 -> x0, waiting for transfers between devices: 55.9 us -> none  [body(): lax.psum_scatter(partial_terms, 'elem', scatter_dimension=1, tiled=True)]
    ppermute x10 -> x0, waiting for transfers between devices: 53.3 us -> none  [the longest x5 30 us: extended_2(): lax.ppermute(lax.slice_in_dim(block, block.shape[dim] - width, None, axis...]
    gather x5 -> x0, local copies, waits for them, and re-layouts: 47 us -> none  [apply_blocks(): picked = jnp.take(flat, table, axis=1)]
    ppermute x10 -> x0, starting transfers between devices: 22.7 us -> none  [the longest x5 17 us: extended_2(): lax.ppermute(lax.slice_in_dim(block, block.shape[dim] - width, None, axis...]
    all_gather x1 -> x0, waiting for transfers between devices: 17 us -> none  [body(): piece = lax.all_gather(current, 'band', axis=0, tiled=True)]
    unnamed x10 -> x7, local copies, waits for them, and re-layouts: 0.02 us -> 4.95 us
  transfers between devices with their start and end apart: 12 -> 0, of which waited for: 12 -> 0; matrix products, arithmetic and copies ran while one was open for 4% -> 0% of each run, Pallas kernels for 0% -> 0%
where the time goes in v1:
time: 123 us; the launch traced here: 122 us
  Pallas kernels  115 us (93%)
  local copies, waits for them, and re-layouts  5.73 us (5%)
    pallas_call x1, Pallas kernels, body(): pl.pallas_call(functools.partial(kernel, geom), out_shape=(jax.ShapeDtype...  115 us
    unnamed x7, local copies, waits for them, and re-layouts  4.95 us

profile of v1, /device:TPU:0, one launch (start us, length us, event | category | flops | bytes accessed | tf_op | source)
XLA Modules:
  0.0 122.4 jit_solution(2462448131166719210)
XLA Ops:
  0.6 0.7 fusion.1
  1.4 0.1 add_add_fusion
  1.5 0.1 copy.7
  1.6 0.7 reshape.18.tab
  2.2 115.2 %shard_map.58 = (bf16[32,128,160]{2,1,0:T(8,128)(2,1)}, f32[16,128]{1,0:T(8,128)}, f32[16,128]{1,0:T(8,128)}) custom-call(s32[192]{0:T(256)} %reshape.18.tab, bf16[32,160,128]{2,1,0:T(8,128)(2,1)} %bitcast.19, bf16[224,160,160]{2,1,0:T(8,128)(2,1)} %bitcast.17), custom_call_target="tpu_custom_call" | custom-call | tf_op jit(solution)/shard_map/pallas_call | solution.py:277
  117.4 0.0 copy-start.1
  117.4 0.0 copy-start
  117.4 3.7 %copy.8 = bf16[128,2,16,160]{0,3,2,1:T(8,128)(2,1)} copy(bf16[128,2,16,160]{3,0,2,1:T(8,128)(2,1)} %bitcast.18) | data formatting | bytes 2621440
  121.2 0.0 copy-done.1
  121.2 0.6 copy.11
  121.8 0.0 copy-done
  121.8 0.6 copy.12
  (2 shorter events, 0.0 us)
Async XLA Ops:
  117.4 3.8 %copy-start.1 = (f32[16,128]{1,0:T(8,128)S(1)}, f32[16,128]{1,0:T(8,128)}, u32[]{:S(2)}) copy-start(f32[16,128]{1,0:T(8,128)} %get-tuple-element.29) | copy-start | bytes 24580
  117.4 4.4 %copy-start = (f32[16,128]{1,0:T(8,128)S(1)}, f32[16,128]{1,0:T(8,128)}, u32[]{:S(2)}) copy-start(f32[16,128]{1,0:T(8,128)} %get-tuple-element.30) | copy-start | bytes 24580

commit v2 on v1

--- a/solution.py
+++ b/solution.py
@@ -8,6 +8,8 @@
 from jax.sharding import PartitionSpec as P
 
 DEGREE = 4
+FAR = 2
+LATE = 2
 MESH = pl.DeviceIdType.MESH
 F32 = jnp.float32
 BF16 = jnp.bfloat16
@@ -19,20 +21,21 @@
 
 def kernel(
     geom,
-    tab,
+    nbr,
     y0,
     ham_hbm,
-    ft,
+    f_out,
     s_out,
     p_out,
     ham,
     buf_a,
     buf_b,
-    lo0,
-    lo1,
-    hi0,
-    hi1,
+    near0,
+    near1,
+    far0,
+    far1,
     acc,
+    ft,
     it,
     others,
     parts,
@@ -40,8 +43,11 @@
     mid,
     got2,
     ham_sem,
-    send_sem,
-    recv_sem,
+    out_sem,
+    near_send,
+    near_recv,
+    far_send,
+    far_recv,
     fsend,
     frecv,
     r1send,
@@ -78,40 +84,42 @@
         pl.semaphore_signal(barrier, inc=1, device_id=peer, device_id_type=MESH)
     pl.semaphore_wait(barrier, len(peers))
 
-    los, his = (lo0, lo1), (hi0, hi1)
-
-    def send_up(step, source):
-        copy = pltpu.make_async_remote_copy(
-            src_ref=source.at[pl.ds(cells, cells)],
-            dst_ref=los[step % 2],
-            send_sem=send_sem.at[step, 0],
-            recv_sem=recv_sem.at[step, 0],
-            device_id={"elem": right},
+    core = me % 2
+    near_base, far_base = (1 - core) * cells, core * cells
+    near_face, far_face = 6 - core, 5 + core
+    near_peer = me + 1 - 2 * core
+    far_peer = lax.rem(me + n - 1 + 2 * core, n)
+    nears, fars = (near0, near1), (far0, far1)
+    piece = cells // FAR
+
+    def near_copy(step, source):
+        return pltpu.make_async_remote_copy(
+            src_ref=source.at[pl.ds(near_base, cells)],
+            dst_ref=nears[step % 2],
+            send_sem=near_send.at[step],
+            recv_sem=near_recv.at[step],
+            device_id={"elem": near_peer},
             device_id_type=MESH,
         )
-        copy.start()
-        return copy
-
-    def send_down(step, source):
-        copy = pltpu.make_async_remote_copy(
-            src_ref=source.at[pl.ds(0, cells)],
-            dst_ref=his[step % 2],
-            send_sem=send_sem.at[step, 1],
-            recv_sem=recv_sem.at[step, 1],
-            device_id={"elem": left},
+
+    def far_copy(step, source, c):
+        return pltpu.make_async_remote_copy(
+            src_ref=source.at[pl.ds(far_base + c * piece, piece)],
+            dst_ref=fars[step % 2].at[pl.ds(c * piece, piece)],
+            send_sem=far_send.at[step, c],
+            recv_sem=far_recv.at[step, c],
+            device_id={"elem": far_peer},
             device_id_type=MESH,
         )
-        copy.start()
-        return copy
 
     fcopies = []
 
-    def send_field(layer):
-        window = pl.ds(layer * cells, cells)
+    def send_field(layer, base):
+        window = pl.ds(base, cells)
         for j in range(1, nband):
             copy = pltpu.make_async_remote_copy(
                 src_ref=buf_a.at[window],
-                dst_ref=others.at[j - 1, window],
+                dst_ref=others.at[j - 1, layer],
                 send_sem=fsend.at[j - 1, layer],
                 recv_sem=frecv.at[j - 1, layer],
                 device_id={"band": lax.rem(bme + j, nband)},
@@ -120,9 +128,24 @@
             copy.start()
             fcopies.append((j, layer, copy))
 
-    up, down = send_up(0, y0), send_down(0, y0)
-    for hc in hcopies:
+    late = (member == 0) | (member == n1 - 1)
+    near = near_copy(0, y0)
+    far = [far_copy(0, y0, c) for c in range(FAR)]
+
+    @pl.when(jnp.logical_not(late))
+    def _():
+        for copy in far:
+            copy.start()
+
+    near.start()
+    for c, hc in enumerate(hcopies):
         hc.wait()
+        if c == LATE:
+
+            @pl.when(late)
+            def _():
+                for copy in far:
+                    copy.start()
 
     current = y0
     for step in range(DEGREE + 1):
@@ -131,64 +154,82 @@
         prior = y0 if step == 1 else target
 
         def local(e, carry, current=current):
-            six = e // cells
-            base = e * 7
+            layer, cell = e // cells, e % cells
+            base, own = e * 7, layer * cells
             total_ = dot(ham[base], current[e])
             for d in range(4):
-                total_ += dot(ham[base + d + 1], current[tab[e * 6 + d]])
-            total_ += dot(ham[base + 6 - six], current[tab[e * 6 + 4]])
+                total_ += dot(
+                    ham[base + d + 1], current[own + lax.rem(nbr[d, layer, cell], cells)]
+                )
+            there = cells - own + lax.rem(nbr[5 - layer, layer, cell], cells)
+            total_ += dot(ham[base + 6 - layer], current[there])
             acc[e] = total_
             return carry
 
         lax.fori_loop(0, total, local, 0)
 
-        def finish(e, carry, step=step, halo=None, face=0, target=target, prior=prior):
-            value = acc[e] + dot(ham[e * 7 + face], halo[tab[e * 6 + 5]])
+        def finish(i, carry, halo, base, face, step=step, target=target, prior=prior):
+            e = base + i
+            index = lax.rem(nbr[face - 1, base // cells, i], cells)
+            value = acc[e] + dot(ham[e * 7 + face], halo[index])
             if step > 0 and step < DEGREE:
                 value = 2.0 * value - prior[e].astype(F32)
             if step < DEGREE:
                 target[e] = value.astype(BF16)
-            if step == DEGREE:
+            else:
                 it[e] = value.T.astype(BF16)
             return carry
 
-        up_next = down_next = None
-        down.wait_recv()
-        lax.fori_loop(
-            cells, total, functools.partial(finish, halo=his[step % 2], face=6), 0
-        )
+        near.wait_recv()
+        at_near = functools.partial(
+            finish, halo=nears[step % 2], base=near_base, face=near_face
+        )
+        at_far = functools.partial(
+            finish, halo=fars[step % 2], base=far_base, face=far_face
+        )
+        near_next, far_next = None, []
+        lax.fori_loop(0, cells, at_near, 0)
         if not last:
-            up_next = send_up(step + 1, target)
+            near_next = near_copy(step + 1, target)
+            near_next.start()
         if step == DEGREE - 1:
-            send_field(1)
-        up.wait_recv()
-        lax.fori_loop(
-            0, cells, functools.partial(finish, halo=los[step % 2], face=5), 0
-        )
-        if not last:
-            down_next = send_down(step + 1, target)
+            send_field(0, near_base)
+        for copy in far:
+            copy.wait_recv()
+        if last:
+            lax.fori_loop(0, cells, at_far, 0)
+        else:
+            for c in range(FAR):
+                lax.fori_loop(c * piece, (c + 1) * piece, at_far, 0)
+                copy = far_copy(step + 1, target, c)
+                copy.start()
+                far_next.append(copy)
         if step == DEGREE - 1:
-            send_field(0)
+            send_field(1, far_base)
+            written = pltpu.make_async_copy(buf_a, f_out, out_sem)
+            written.start()
 
             def turn(e, carry):
                 ft[e] = buf_a[e].astype(F32).T.astype(BF16)
                 return carry
 
             lax.fori_loop(0, total, turn, 0)
-        up.wait_send()
-        down.wait_send()
-        up, down = up_next, down_next
+        near.wait_send()
+        for copy in far:
+            copy.wait_send()
+        near, far = near_next, far_next
         current = target
 
     per = bands // rows
 
     def gram(field, first, count, state):
-        def body(e, carry):
+        def body(i, carry):
             s, p = carry
-            v = field(e)
+            v = field(i)
+            e = first + i
             return s + dot(ft[e], v), p + dot(it[e], v)
 
-        return lax.fori_loop(first, first + count, body, state)
+        return lax.fori_loop(0, count, body, state)
 
     def put(who, state):
         for t in range(2):
@@ -204,7 +245,8 @@
         for jj, layer, copy in fcopies:
             if jj == j:
                 copy.wait_recv()
-                state = gram(lambda e: others[j - 1, e], layer * cells, cells, state)
+                base = near_base if layer == 0 else far_base
+                state = gram(lambda i: others[j - 1, layer, i], base, cells, state)
         put(lax.rem(bme + nband - j, nband), state)
 
     copies = []
@@ -248,6 +290,7 @@
         final += got2[j]
     for copy in copies2:
         copy.wait_send()
+    written.wait()
     s_out[...] = final[0] * factor
     p_out[...] = final[1] * factor
 
@@ -259,13 +302,7 @@
     rows = bands * nband // n
     n1 = 4
     n2 = n // n1
-    first = lax.axis_index("elem") * layers
-    layer_of = neighbours // cells
-    cell_of = neighbours % cells
-    inside = (layer_of - first) % depth * cells + cell_of
-    low = jnp.concatenate([inside[0, :, :4], inside[0, :, 5:6], cell_of[0, :, 4:5]], axis=1)
-    high = jnp.concatenate([inside[1, :, :4], inside[1, :, 4:5], cell_of[1, :, 5:6]], axis=1)
-    tab = jnp.concatenate([low, high], axis=0).reshape(-1)
+    nbr = neighbours.transpose(2, 0, 1)
     y0 = basis.reshape(bands, total, funcs).transpose(1, 2, 0)
     ham = hamiltonian.reshape(total * 7, funcs, funcs)
     factor = 1.0 / (depth * cells * funcs)
@@ -274,15 +311,15 @@
     half = (cells, funcs, bands)
     dma = pltpu.SemaphoreType.DMA
     small = jax.ShapeDtypeStruct((rows, bands), F32)
-    ft, s, p = pl.pallas_call(
+    field, s, p = pl.pallas_call(
         functools.partial(kernel, geom),
-        out_shape=(jax.ShapeDtypeStruct((total, bands, funcs), BF16), small, small),
+        out_shape=(jax.ShapeDtypeStruct((total, funcs, bands), BF16), small, small),
         in_specs=[
             pl.BlockSpec(memory_space=pltpu.SMEM),
             vm,
             pl.BlockSpec(memory_space=pl.ANY),
         ],
-        out_specs=(vm, vm, vm),
+        out_specs=(pl.BlockSpec(memory_space=pl.ANY), vm, vm),
         scratch_shapes=[
             pltpu.VMEM((total * 7, funcs, funcs), BF16),
             pltpu.VMEM((total, funcs, bands), BF16),
@@ -293,14 +330,18 @@
             pltpu.VMEM(half, BF16),
             pltpu.VMEM((total, funcs, bands), F32),
             pltpu.VMEM((total, bands, funcs), BF16),
-            pltpu.VMEM((nband - 1, total, funcs, bands), BF16),
+            pltpu.VMEM((total, bands, funcs), BF16),
+            pltpu.VMEM((nband - 1, 2, cells, funcs, bands), BF16),
             pltpu.VMEM((n1, n2, 2, rows, bands), F32),
             pltpu.VMEM((n1 - 1, n2, 2, rows, bands), F32),
             pltpu.VMEM((n2, 2, rows, bands), F32),
             pltpu.VMEM((n2 - 1, 2, rows, bands), F32),
             dma((4,)),
-            dma((DEGREE + 1, 2)),
-            dma((DEGREE + 1, 2)),
+            dma,
+            dma((DEGREE + 1,)),
+            dma((DEGREE + 1,)),
+            dma((DEGREE + 1, FAR)),
+            dma((DEGREE + 1, FAR)),
             dma((nband - 1, 2)),
             dma((nband - 1, 2)),
             dma((n1 - 1,)),
@@ -311,8 +352,8 @@
         compiler_params=pltpu.CompilerParams(
             collective_id=0, has_side_effects=True, vmem_limit_bytes=56 * 1024 * 1024
         ),
-    )(tab, y0, ham)
-    filtered = ft.transpose(1, 0, 2).reshape(bands, layers, cells, funcs)
+    )(nbr, y0, ham)
+    filtered = field.transpose(2, 0, 1).reshape(bands, layers, cells, funcs)
     return filtered, s, p
 
 

time: 123 us -> 119 us (0.967)
  local copies, waits for them, and re-layouts: 5.73 us -> 3.67 us
    unnamed x7, local copies, waits for them, and re-layouts: 4.95 us -> 3.67 us
where the time goes in v2:
time: 119 us
  Pallas kernels  114 us (96%)
  local copies, waits for them, and re-layouts  3.67 us (3%)
    pallas_call x1, Pallas kernels, body(): pl.pallas_call(functools.partial(kernel, geom), out_shape=(jax.ShapeDtype...  114 us
    unnamed x7, local copies, waits for them, and re-layouts  3.67 us

profile of v2, /device:TPU:0, one launch (start us, length us, event | category | flops | bytes accessed | tf_op | source)
XLA Modules:
  0.0 118.6 jit_solution(10824445506408223311)
XLA Ops:
  0.6 114.3 %shard_map.58 = (bf16[32,160,128]{2,1,0:T(8,128)(2,1)}, f32[16,128]{1,0:T(8,128)}, f32[16,128]{1,0:T(8,128)}) custom-call(s32[6,2,16]{2,1,0:T(2,128)} %bitcast.11, bf16[32,160,128]{2,1,0:T(8,128)(2,1)} %bitcast.9, bf16[224,160,160]{2,1,0:T(8,128)(2,1)} %bitcast.8), custom_call_target="tpu_custom_call" | custom-call | tf_op jit(solution)/shard_map/pallas_call | solution.py:314
  114.9 0.0 copy-start.1
  114.9 0.0 copy-start
  114.9 2.5 %copy.9 = bf16[128,2,16,160]{0,3,2,1:T(8,128)(2,1)} copy(bf16[128,2,16,160]{0,3,2,1:T(8,128)(2,1)} %bitcast.10) | data formatting | bytes 2621440
  117.4 0.0 copy-done.1
  117.4 0.6 copy.10
  118.0 0.0 copy-done
  118.0 0.6 copy.11
Async XLA Ops:
  114.9 2.5 %copy-start.1 = (f32[16,128]{1,0:T(8,128)S(1)}, f32[16,128]{1,0:T(8,128)}, u32[]{:S(2)}) copy-start(f32[16,128]{1,0:T(8,128)} %get-tuple-element.13) | copy-start | bytes 24580
  114.9 3.1 %copy-start = (f32[16,128]{1,0:T(8,128)S(1)}, f32[16,128]{1,0:T(8,128)}, u32[]{:S(2)}) copy-start(f32[16,128]{1,0:T(8,128)} %get-tuple-element.14) | copy-start | bytes 24580

commit v3 on v2

--- a/solution.py
+++ b/solution.py
@@ -166,7 +166,7 @@
             acc[e] = total_
             return carry
 
-        lax.fori_loop(0, total, local, 0)
+        lax.fori_loop(0, total, local, 0, unroll=4)
 
         def finish(i, carry, halo, base, face, step=step, target=target, prior=prior):
             e = base + i
@@ -188,7 +188,7 @@
             finish, halo=fars[step % 2], base=far_base, face=far_face
         )
         near_next, far_next = None, []
-        lax.fori_loop(0, cells, at_near, 0)
+        lax.fori_loop(0, cells, at_near, 0, unroll=4)
         if not last:
             near_next = near_copy(step + 1, target)
             near_next.start()
@@ -197,10 +197,10 @@
         for copy in far:
             copy.wait_recv()
         if last:
-            lax.fori_loop(0, cells, at_far, 0)
+            lax.fori_loop(0, cells, at_far, 0, unroll=4)
         else:
             for c in range(FAR):
-                lax.fori_loop(c * piece, (c + 1) * piece, at_far, 0)
+                lax.fori_loop(c * piece, (c + 1) * piece, at_far, 0, unroll=4)
                 copy = far_copy(step + 1, target, c)
                 copy.start()
                 far_next.append(copy)
@@ -213,7 +213,7 @@
                 ft[e] = buf_a[e].astype(F32).T.astype(BF16)
                 return carry
 
-            lax.fori_loop(0, total, turn, 0)
+            lax.fori_loop(0, total, turn, 0, unroll=4)
         near.wait_send()
         for copy in far:
             copy.wait_send()
@@ -229,7 +229,7 @@
             e = first + i
             return s + dot(ft[e], v), p + dot(it[e], v)
 
-        return lax.fori_loop(0, count, body, state)
+        return lax.fori_loop(0, count, body, state, unroll=4)
 
     def put(who, state):
         for t in range(2):

time: 119 us -> 108 us (0.908)
  Pallas kernels: 114 us -> 103 us
    pallas_call x1, Pallas kernels: 114 us -> 103 us  [body(): pl.pallas_call(functools.partial(kernel, geom), out_shape=(jax.ShapeDtype...]
where the time goes in v3:
time: 108 us; the launch traced here: 107 us
  Pallas kernels  103 us (95%)
  local copies, waits for them, and re-layouts  3.67 us (3%)
    pallas_call x1, Pallas kernels, body(): pl.pallas_call(functools.partial(kernel, geom), out_shape=(jax.ShapeDtype...  103 us
    unnamed x7, local copies, waits for them, and re-layouts  3.67 us

profile of v3, /device:TPU:0, one launch (start us, length us, event | category | flops | bytes accessed | tf_op | source)
XLA Modules:
  0.0 107.3 jit_solution(13896115046468341341)
XLA Ops:
  0.6 103.0 %shard_map.58 = (bf16[32,160,128]{2,1,0:T(8,128)(2,1)}, f32[16,128]{1,0:T(8,128)}, f32[16,128]{1,0:T(8,128)}) custom-call(s32[6,2,16]{2,1,0:T(2,128)} %bitcast.11, bf16[32,160,128]{2,1,0:T(8,128)(2,1)} %bitcast.9, bf16[224,160,160]{2,1,0:T(8,128)(2,1)} %bitcast.8), custom_call_target="tpu_custom_call" | custom-call | tf_op jit(solution)/shard_map/pallas_call | solution.py:314
  103.6 0.0 copy-start.1
  103.7 0.0 copy-start
  103.7 2.5 %copy.9 = bf16[128,2,16,160]{0,3,2,1:T(8,128)(2,1)} copy(bf16[128,2,16,160]{0,3,2,1:T(8,128)(2,1)} %bitcast.10) | data formatting | bytes 2621440
  106.1 0.0 copy-done.1
  106.1 0.6 copy.10
  106.7 0.0 copy-done
  106.7 0.6 copy.11
Async XLA Ops:
  103.6 2.5 %copy-start.1 = (f32[16,128]{1,0:T(8,128)S(1)}, f32[16,128]{1,0:T(8,128)}, u32[]{:S(2)}) copy-start(f32[16,128]{1,0:T(8,128)} %get-tuple-element.13) | copy-start | bytes 24580
  103.7 3.1 %copy-start = (f32[16,128]{1,0:T(8,128)S(1)}, f32[16,128]{1,0:T(8,128)}, u32[]{:S(2)}) copy-start(f32[16,128]{1,0:T(8,128)} %get-tuple-element.14) | copy-start | bytes 24580
